TPU v7x, 32 devices: a whole 2x2x4 slice. The times are simulated.
32 devices in a mesh: tm: 4 (over y, core), dom: 8 (over z, x).
Axes of the slice: x: 2, y: 2, z: 4, core: 2. Of those that a mesh axis runs over, the one named last changes fastest.
Arguments:
- particles: float32 [4, 64, 4096], P('tm', None, 'dom'), may hold values from -12 to 12, as said below
- noise: float32 [4, 64, 4096], P('tm', None, 'dom'), may hold values from -6 to 6
Outputs:
- advanced: float32 [4, 64, 4096], P('tm', None, 'dom')
Inputs may be any that keep to these rules, and one draw needn't show every extreme that they name: `particles`: positions of cells in principal components, each time point about a shifted centre.
All inputs are finite; a program needn't handle non-finite values.
Results may differ from a plain program's by a relative error of at most 0.012.
The roundings to bfloat16 on the way count: a program that leaves them out, or rounds other values in their place, can miss the bound.
Values may be sent and summed in bfloat16 or wider, within the bound.
A program may use at most 64 MiB of HBM per device.

v0:
```python
import math
import jax
import jax.numpy as jnp
from jax import lax
from jax.sharding import PartitionSpec as P

SWEEPS = 2
EPS = 4.0
STEP = 0.5
TEMP = 0.05


def passed_along(value, axis, steps):
    count = lax.axis_size(axis)
    leading, last = (max(0, -steps), min(count, count - steps))
    return lax.ppermute(value, axis, [(source, source + steps) for source in range(leading, last)])


def col_tiles(targets, potential):
    features = targets.shape[0]
    col_count = targets.shape[1]
    tile_width = math.gcd(col_count, 1024)
    tile_count = col_count // tile_width
    tiles = targets.reshape(features, tile_count, tile_width).transpose(1, 0, 2)
    return (tiles, potential.reshape(tile_count, tile_width))


def tile_scores(sources, target_tile, pot_tile):
    products = lax.dot_general(
        sources, target_tile, (((0,), (0,)), ((), ())), preferred_element_type=jnp.float32
    )
    return (products + pot_tile[None, :]) / EPS


def log_totals(sources, tiles, pot_tiles):
    row_count = sources.shape[1]

    def log_advance(carry, pieces):
        highest, totals = carry
        scores = tile_scores(sources, pieces[0], pieces[1])
        merged = jnp.maximum(highest, jnp.max(scores, axis=1))
        totals = totals * jnp.exp(highest - merged) + jnp.sum(
            jnp.exp(scores - merged[:, None]), axis=1
        )
        return ((merged, totals), None)

    start = (jnp.full((row_count,), -jnp.inf, jnp.float32), jnp.zeros((row_count,), jnp.float32))
    (highest, totals), unused = lax.scan(log_advance, start, (tiles, pot_tiles))
    return (highest, totals)


def update(sources, targets, potential):
    tiles, pot_tiles = col_tiles(targets, potential)
    highest, totals = log_totals(sources, tiles, pot_tiles)
    result = -EPS * (highest + jnp.log(totals)) + EPS * math.log(targets.shape[1])
    return (result, highest, totals)


def barycentre(sources, targets, potential, highest, totals):
    tiles, pot_tiles = col_tiles(targets, potential)

    def barycentre_advance(summed, pieces):
        scores = tile_scores(sources, pieces[0], pieces[1])
        weights = (jnp.exp(scores - highest[:, None]) / totals[:, None]).astype(jnp.bfloat16)
        summed = summed + lax.dot_general(
            pieces[0], weights, (((1,), (1,)), ((), ())), preferred_element_type=jnp.float32
        )
        return (summed, None)

    start = jnp.zeros((targets.shape[0], sources.shape[1]), jnp.float32)
    summed, unused = lax.scan(barycentre_advance, start, (tiles, pot_tiles))
    return summed


def neighbours(own_block):
    gathered = lax.all_gather(own_block, "dom", axis=1, tiled=True)
    next_all = passed_along(gathered, "tm", -1)
    prev_all = passed_along(gathered, "tm", 1)
    return (next_all, prev_all)


def potentials_from(values, offset):
    gathered = lax.all_gather(values, "dom", axis=0, tiled=True)
    return passed_along(gathered, "tm", offset)


def per_device(particles, noise):
    points = particles[0]
    rounded = points.astype(jnp.bfloat16)
    next_all, prev_all = neighbours(rounded)
    time_index = lax.axis_index("tm")
    last_time = lax.axis_size("tm") - 1
    next_pot = -0.5 * jnp.sum(jnp.square(next_all.astype(jnp.float32)), axis=0)
    for sweep_index in range(SWEEPS):
        if sweep_index > 0:
            next_pot = potentials_from(target_pot, -1)
        source_pot, unused_high, unused_totals = update(rounded, next_all, next_pot)
        prev_pot = potentials_from(source_pot, 1)
        target_pot, prev_high, prev_totals = update(rounded, prev_all, prev_pot)
    next_pot = potentials_from(target_pot, -1)
    next_tiles, next_pot_tiles = col_tiles(next_all, next_pot)
    next_high, next_totals = log_totals(rounded, next_tiles, next_pot_tiles)
    bary_next = barycentre(rounded, next_all, next_pot, next_high, next_totals)
    bary_prev = barycentre(rounded, prev_all, prev_pot, prev_high, prev_totals)
    pull_next = jnp.where(time_index < last_time, points - bary_next, 0.0)
    pull_prev = jnp.where(time_index > 0, points - bary_prev, 0.0)
    advanced = points - STEP * (pull_next + pull_prev) + math.sqrt(2.0 * STEP * TEMP) * noise[0]
    return advanced[None]


def solution(mesh):
    in_specs = (P("tm", None, "dom"), P("tm", None, "dom"))
    out_specs = P("tm", None, "dom")
    return jax.shard_map(
        per_device, mesh=mesh, in_specs=in_specs, out_specs=out_specs, check_vma=False
    )
```

profile of v0, /device:TPU:5, one launch (start us, length us, event | category | flops | bytes accessed | tf_op | source)
XLA Modules:
  0.0 191.1 jit_solution(3282749936282625119)
XLA Ops:
  0.0 0.9 bitcast_convert_fusion
  0.9 26.1 %all_gather.15 = bf16[64,4096]{1,0:T(8,128)(2,1)S(1)} all-gather(bf16[64,512]{1,0:T(8,128)(2,1)S(1)} %bitcast_convert_fusion), channel_id=1, replica_groups=mesh['tm'=4,'dom'=8] {'dom'}, dimensions={1}, use_global_device_ids=true | all-gather | bytes 589824 | tf_op jit(solution)/shard_map/all_gather | solution.py:76
  27.0 8.0 %collective-permute-start = (bf16[64,4096]{1,0:T(8,128)(2,1)S(1)}, bf16[64,4096]{1,0:T(8,128)(2,1)S(1)}, u32[]{:S(2)}, u32[]{:S(2)}) collective-permute-start(bf16[64,4096]{1,0:T(8,128)(2,1)S(1)} %all_gather.15), channel_id=1, source_target_pairs={{8,0},{16,8},{24,16},{9,1},{17,9},{25,17},{10,2},{18,10},{26,18},{... | collective-permute-start | bytes 1572872 | tf_op jit(solution)/shard_map/ppermute | solution.py:16
  35.1 1.3 collective-permute-start.1
  36.8 4.3 %while.87 = (s32[]{:T(128)}, f32[512]{0:T(512)S(1)}, f32[512]{0:T(512)S(1)}, bf16[4,64,1024]{2,1,0:T(8,128)(2,1)S(1)}, bf16[64,512]{1,0:T(8,128)(2,1)S(1)}, /*index=5*/f32[4,1024]{1,0:T(4,128)S(1)}, s32[]{:T(128)}, s32[]{:T(128)}) while((s32[]{:T(128)}, f32[512]{0:T(512)S(1)}, f32[512]{0:T(512)S(1)}, ...), condition=%wide.region_4.5_spmd.clone, body=%wide.region_1.4_spmd.clone.sunk | while | flops 70781440 | bytes 4434024 | solution.py:48
  36.8 0.5 fusion.92
  37.3 0.5 exponential_reduce_fusion.10
  37.9 0.5 fusion.92
  38.4 0.5 exponential_reduce_fusion.10
  39.0 0.5 fusion.92
  39.5 0.5 exponential_reduce_fusion.10
  40.0 0.5 fusion.92
  40.6 0.5 exponential_reduce_fusion.10
  41.1 21.5 %all-gather = f32[8,1,512]{2,1,0:T(1,128)S(1)} all-gather(f32[1,1,512]{2,1,0:T(1,128)S(1)} %bitcast.159), channel_id=1, replica_groups=mesh['tm'=4,'dom'=8] {'dom'}, dimensions={0}, use_global_device_ids=true | all-gather | bytes 18432 | tf_op jit(solution)/shard_map/all_gather | solution.py:83
  62.6 1.3 collective-permute-start.2
  63.9 1.1 copy.11
  65.0 9.9 %collective-permute-done.2 = f32[4096]{0:T(1024)S(1)} collective-permute-done((f32[4096]{0:T(1024)S(1)}, f32[4096]{0:T(1024)S(1)}, u32[]{:S(2)}, u32[]{:S(2)}) %collective-permute-start.2) | collective-permute-done | bytes 16416 | tf_op jit(solution)/shard_map/ppermute | solution.py:16
  75.0 4.3 %while.88 = (s32[]{:T(128)}, f32[512]{0:T(512)S(1)}, f32[512]{0:T(512)S(1)}, bf16[4,64,1024]{2,1,0:T(8,128)(2,1)S(1)}, bf16[64,512]{1,0:T(8,128)(2,1)S(1)}, /*index=5*/f32[4,1024]{1,0:T(4,128)S(1)}, s32[]{:T(128)}, s32[]{:T(128)}) while((s32[]{:T(128)}, f32[512]{0:T(512)S(1)}, f32[512]{0:T(512)S(1)}, ...), condition=%wide.region_8.9_spmd.clone, body=%wide.region_5.8_spmd.clone.sunk | while | flops 70781440 | bytes 4434024 | solution.py:48
  75.5 0.5 exponential_reduce_fusion.11
  76.1 0.5 fusion.95
  76.6 0.5 exponential_reduce_fusion.11
  77.1 0.5 fusion.95
  77.7 0.5 exponential_reduce_fusion.11
  78.7 0.5 exponential_reduce_fusion.11
  79.3 21.5 %all-gather.1 = f32[8,1,512]{2,1,0:T(1,128)S(1)} all-gather(f32[1,1,512]{2,1,0:T(1,128)S(1)} %bitcast.160), channel_id=1, replica_groups=mesh['tm'=4,'dom'=8] {'dom'}, dimensions={0}, use_global_device_ids=true | all-gather | bytes 18432 | tf_op jit(solution)/shard_map/all_gather | solution.py:83
  100.8 9.0 %collective-permute-start.3 = (f32[4096]{0:T(1024)S(1)}, f32[4096]{0:T(1024)S(1)}, u32[]{:S(2)}, u32[]{:S(2)}) collective-permute-start(f32[4096]{0:T(1024)S(1)} %bitcast.158), channel_id=1, source_target_pairs={{8,0},{16,8},{24,16},{9,1},{17,9},{25,17},{10,2},{18,10},{26,18},{... | collective-permute-start | bytes 49160 | tf_op jit(solution)/shard_map/ppermute | solution.py:16
  109.8 0.8 collective-permute-done.3
  110.6 4.3 %while.89 = (s32[]{:T(128)}, f32[512]{0:T(512)S(1)}, f32[512]{0:T(512)S(1)}, bf16[4,64,1024]{2,1,0:T(8,128)(2,1)S(1)}, bf16[64,512]{1,0:T(8,128)(2,1)S(1)}, /*index=5*/f32[4,1024]{1,0:T(4,128)S(1)}, s32[]{:T(128)}, s32[]{:T(128)}) while((s32[]{:T(128)}, f32[512]{0:T(512)S(1)}, f32[512]{0:T(512)S(1)}, ...), condition=%wide.region_12.13_spmd.clone, body=%wide.region_9.12_spmd.clone.sunk | while | flops 70781440 | bytes 4434024 | solution.py:48
  111.1 0.5 exponential_reduce_fusion.12
  111.7 0.5 fusion.98
  112.2 0.5 exponential_reduce_fusion.12
  112.8 0.5 fusion.98
  113.3 0.5 exponential_reduce_fusion.12
  114.4 0.5 exponential_reduce_fusion.12
  114.9 21.5 %all-gather.2 = f32[8,1,512]{2,1,0:T(1,128)S(1)} all-gather(f32[1,1,512]{2,1,0:T(1,128)S(1)} %bitcast.161), channel_id=1, replica_groups=mesh['tm'=4,'dom'=8] {'dom'}, dimensions={0}, use_global_device_ids=true | all-gather | bytes 18432 | tf_op jit(solution)/shard_map/all_gather | solution.py:83
  136.4 1.3 collective-permute-start.4
  137.8 6.4 %collective-permute-done.4 = f32[4096]{0:T(1024)S(1)} collective-permute-done((f32[4096]{0:T(1024)S(1)}, f32[4096]{0:T(1024)S(1)}, u32[]{:S(2)}, u32[]{:S(2)}) %collective-permute-start.4) | collective-permute-done | bytes 16416 | tf_op jit(solution)/shard_map/ppermute | solution.py:16
  144.2 4.3 %while.90 = (s32[]{:T(128)}, f32[512]{0:T(512)S(1)}, f32[512]{0:T(512)S(1)}, bf16[4,64,1024]{2,1,0:T(8,128)(2,1)S(1)}, bf16[64,512]{1,0:T(8,128)(2,1)S(1)}, /*index=5*/f32[4,1024]{1,0:T(4,128)S(1)}, s32[]{:T(128)}, s32[]{:T(128)}) while((s32[]{:T(128)}, f32[512]{0:T(512)S(1)}, f32[512]{0:T(512)S(1)}, ...), condition=%wide.region_16.17_spmd.clone, body=%wide.region_13.16_spmd.clone.sunk | while | flops 70781440 | bytes 4434024 | solution.py:48
  144.2 0.5 fusion.101
  144.8 0.5 exponential_reduce_fusion.13
  145.8 0.5 exponential_reduce_fusion.13
  146.9 0.5 exponential_reduce_fusion.13
  148.0 0.5 exponential_reduce_fusion.13
  148.5 21.5 %all-gather.3 = f32[8,1,512]{2,1,0:T(1,128)S(1)} all-gather(f32[1,1,512]{2,1,0:T(1,128)S(1)} %bitcast.162), channel_id=1, replica_groups=mesh['tm'=4,'dom'=8] {'dom'}, dimensions={0}, use_global_device_ids=true | all-gather | bytes 18432 | tf_op jit(solution)/shard_map/all_gather | solution.py:83
  170.0 9.0 %collective-permute-start.5 = (f32[4096]{0:T(1024)S(1)}, f32[4096]{0:T(1024)S(1)}, u32[]{:S(2)}, u32[]{:S(2)}) collective-permute-start(f32[4096]{0:T(1024)S(1)} %bitcast.155), channel_id=1, source_target_pairs={{8,0},{16,8},{24,16},{9,1},{17,9},{25,17},{10,2},{18,10},{26,18},{... | collective-permute-start | bytes 49160 | tf_op jit(solution)/shard_map/ppermute | solution.py:16
  179.0 3.5 %while.93 = (s32[]{:T(128)}, f32[64,512]{1,0:T(8,128)S(1)}, bf16[4,64,1024]{2,1,0:T(8,128)(2,1)S(1)}, bf16[64,512]{1,0:T(8,128)(2,1)S(1)}, f32[4,1024]{1,0:T(4,1...) while((s32[]{:T(128)}, f32[64,512]{1,0:T(8,128)S(1)}, ...), condition=%wide.region_24.25_spmd.clone, body=%wide.region_23.24_spmd.clone.sunk | while | flops 136904704 | bytes 607339 | solution.py:71
  179.1 0.8 fusion.113
  179.9 0.8 fusion.113
  180.8 0.8 fusion.113
  181.7 0.8 fusion.113
  182.6 4.3 %while.91 = (s32[]{:T(128)}, f32[512]{0:T(512)S(1)}, f32[512]{0:T(512)S(1)}, bf16[4,64,1024]{2,1,0:T(8,128)(2,1)S(1)}, bf16[64,512]{1,0:T(8,128)(2,1)S(1)}, /*index=5*/f32[4,1024]{1,0:T(4,128)S(1)}, s32[]{:T(128)}, s32[]{:T(128)}) while((s32[]{:T(128)}, f32[512]{0:T(512)S(1)}, f32[512]{0:T(512)S(1)}, ...), condition=%wide.region_20.21_spmd.clone, body=%wide.region_17.20_spmd.clone.sunk | while | flops 70781440 | bytes 4434024 | solution.py:48
  182.6 0.5 fusion.104
  183.1 0.5 exponential_reduce_fusion.14
  183.7 0.5 fusion.104
  184.2 0.5 exponential_reduce_fusion.14
  185.3 0.5 exponential_reduce_fusion.14
  185.8 0.5 fusion.104
  186.3 0.5 exponential_reduce_fusion.14
  186.9 3.5 %while.92 = (s32[]{:T(128)}, f32[64,512]{1,0:T(8,128)S(1)}, bf16[4,64,1024]{2,1,0:T(8,128)(2,1)S(1)}, bf16[64,512]{1,0:T(8,128)(2,1)S(1)}, f32[4,1024]{1,0:T(4,1...) while((s32[]{:T(128)}, f32[64,512]{1,0:T(8,128)S(1)}, ...), condition=%wide.region_22.23_spmd.clone, body=%wide.region_21.22_spmd.clone.sunk | while | flops 136904704 | bytes 607339 | solution.py:71
  186.9 0.8 fusion.109
  187.8 0.8 fusion.109
  188.7 0.8 fusion.109
  189.5 0.8 fusion.109
  190.4 0.7 fusion.56
  (127 shorter events, 5.2 us)
Async XLA Ops:
  27.0 9.5 %collective-permute-start = (bf16[64,4096]{1,0:T(8,128)(2,1)S(1)}, bf16[64,4096]{1,0:T(8,128)(2,1)S(1)}, u32[]{:S(2)}, u32[]{:S(2)}) collective-permute-start(bf16[64,4096]{1,0:T(8,128)(2,1)S(1)} %all_gather.15), channel_id=1, source_target_pairs={{8,0},{16,8},{24,16},{9,1},{17,9},{25,17},{10,2},{18,10},{26,18},{... | collective-permute-start | bytes 1572872 | tf_op jit(solution)/shard_map/ppermute | solution.py:16
  35.1 28.8 %collective-permute-start.1 = (bf16[64,4096]{1,0:T(8,128)(2,1)S(1)}, bf16[64,4096]{1,0:T(8,128)(2,1)}, u32[]{:S(2)}, u32[]{:S(2)}) collective-permute-start(bf16[64,4096]{1,0:T(8,128)(2,1)S(1)} %all_gather.15), channel_id=1, source_target_pairs={{0,8},{8,16},{16,24},{1,9},{9,17},{17,25},{2,10},{10,18},{18,26},{... | collective-permute-start | bytes 1572872 | tf_op jit(solution)/shard_map/ppermute | solution.py:16
  62.6 12.3 %collective-permute-start.2 = (f32[4096]{0:T(1024)S(1)}, f32[4096]{0:T(1024)S(1)}, u32[]{:S(2)}, u32[]{:S(2)}) collective-permute-start(f32[4096]{0:T(1024)S(1)} %bitcast.157), channel_id=1, source_target_pairs={{0,8},{8,16},{16,24},{1,9},{9,17},{17,25},{2,10},{10,18},{18,26},{... | collective-permute-start | bytes 49160 | tf_op jit(solution)/shard_map/ppermute | solution.py:16
  100.8 9.8 %collective-permute-start.3 = (f32[4096]{0:T(1024)S(1)}, f32[4096]{0:T(1024)S(1)}, u32[]{:S(2)}, u32[]{:S(2)}) collective-permute-start(f32[4096]{0:T(1024)S(1)} %bitcast.158), channel_id=1, source_target_pairs={{8,0},{16,8},{24,16},{9,1},{17,9},{25,17},{10,2},{18,10},{26,18},{... | collective-permute-start | bytes 49160 | tf_op jit(solution)/shard_map/ppermute | solution.py:16
  136.4 7.8 %collective-permute-start.4 = (f32[4096]{0:T(1024)S(1)}, f32[4096]{0:T(1024)S(1)}, u32[]{:S(2)}, u32[]{:S(2)}) collective-permute-start(f32[4096]{0:T(1024)S(1)} %bitcast.156), channel_id=1, source_target_pairs={{0,8},{8,16},{16,24},{1,9},{9,17},{17,25},{2,10},{10,18},{18,26},{... | collective-permute-start | bytes 49160 | tf_op jit(solution)/shard_map/ppermute | solution.py:16
  170.0 12.5 %collective-permute-start.5 = (f32[4096]{0:T(1024)S(1)}, f32[4096]{0:T(1024)S(1)}, u32[]{:S(2)}, u32[]{:S(2)}) collective-permute-start(f32[4096]{0:T(1024)S(1)} %bitcast.155), channel_id=1, source_target_pairs={{8,0},{16,8},{24,16},{9,1},{17,9},{25,17},{10,2},{18,10},{26,18},{... | collective-permute-start | bytes 49160 | tf_op jit(solution)/shard_map/ppermute | solution.py:16
  186.9 3.5 %copy-start = (f32[1,64,512]{2,1,0:T(8,128)S(1)}, f32[1,64,512]{2,1,0:T(8,128)}, u32[]{:S(2)}) copy-start(f32[1,64,512]{2,1,0:T(8,128)} %param.16) | copy-start | bytes 393220
  186.9 3.5 %copy-start.1 = (f32[1,64,512]{2,1,0:T(8,128)S(1)}, f32[1,64,512]{2,1,0:T(8,128)}, u32[]{:S(2)}) copy-start(f32[1,64,512]{2,1,0:T(8,128)} %param.17) | copy-start | bytes 393220
where the time goes:
time: 191 us
  blocking collectives  112 us (59%)
  starting transfers between devices  29.8 us (16%)
  waiting for transfers between devices  17.3 us (9%)
  matrix products  16.5 us (9%)
  other arithmetic  12.2 us (6%)
    all_gather x4, blocking collectives, potentials_from(): gathered = lax.all_gather(values, 'dom', axis=0, tiled=True)  86.1 us
    ppermute x6, starting transfers between devices, passed_along(): lax.ppermute(value, axis, [(source, source + steps) for source in range(l...  29.8 us
    all_gather x1, blocking collectives, neighbours(): gathered = lax.all_gather(own_block, 'dom', axis=1, tiled=True)  26.1 us
    ppermute x6, waiting for transfers between devices, passed_along(): lax.ppermute(value, axis, [(source, source + steps) for source in range(l...  17.3 us
    reduce_sum x20, other arithmetic, log_advance(): jnp.sum(jnp.exp(scores - merged[:, None]), axis=1)  9.89 us
    dot_general x20, matrix products, tile_scores(): lax.dot_general(sources, target_tile, (((0,), (0,)), ((), ())), preferred...  9.87 us
    dot_general x8, matrix products, barycentre_advance(): lax.dot_general(pieces[0], weights, (((1,), (1,)), ((), ())), preferred_e...  6.65 us
  transfers between devices with their start and end apart: 6, of which 4 were waited for; matrix products, arithmetic and copies ran while one was open for 5% of the time, Pallas kernels for 0%

commit v1 on v0

--- a/solution.py
+++ b/solution.py
@@ -73,7 +73,12 @@
 
 
 def neighbours(own_block):
-    gathered = lax.all_gather(own_block, "dom", axis=1, tiled=True)
+    ring = [own_block]
+    for hop in range(7):
+        ring.append(lax.ppermute(ring[-1], "dom", [(dev, (dev + 1) % 8) for dev in range(8)]))
+    gathered = jnp.roll(
+        jnp.concatenate(ring[::-1], axis=1), (lax.axis_index("dom") + 1) * ring[0].shape[1], axis=1
+    )
     next_all = passed_along(gathered, "tm", -1)
     prev_all = passed_along(gathered, "tm", 1)
     return (next_all, prev_all)

time: 191 us -> 217 us (1.14)
  waiting for transfers between devices: 17.3 us -> 57.9 us
  blocking collectives: 112 us -> 86.1 us
  matrix products: 16.5 us -> 21.8 us
  starting transfers between devices: 29.8 us -> 33.5 us
    ppermute x0 -> x7, waiting for transfers between devices: none -> 40.2 us  [neighbours(): lax.ppermute(ring[-1], 'dom', [(dev, (dev + 1) % 8) for dev in range(8)])]
    all_gather x1 -> x0, blocking collectives: 26.1 us -> none  [neighbours(): gathered = lax.all_gather(own_block, 'dom', axis=1, tiled=True)]
    dot_general x8, matrix products: 6.65 us -> 12 us  [barycentre_advance(): lax.dot_general(pieces[0], weights, (((1,), (1,)), ((), ())), preferred_e...]
    ppermute x6, starting transfers between devices: 29.8 us -> 32.2 us  [passed_along(): lax.ppermute(value, axis, [(source, source + steps) for source in range(l...]
  transfers between devices with their start and end apart: 6 -> 13, of which waited for: 4 -> 11; matrix products, arithmetic and copies ran while one was open for 5% -> 6% of each run, Pallas kernels for 0% -> 0%
where the time goes in v1:
time: 217 us; the launch traced here: 216 us
  blocking collectives  86.1 us (40%)
  waiting for transfers between devices  57.9 us (27%)
  starting transfers between devices  33.5 us (15%)
  matrix products  21.8 us (10%)
  other arithmetic  13.2 us (6%)
  local copies, waits for them, and re-layouts  2.41 us (1%)
    all_gather x4, blocking collectives, potentials_from(): gathered = lax.all_gather(values, 'dom', axis=0, tiled=True)  86.1 us
    ppermute x7, waiting for transfers between devices, neighbours(): lax.ppermute(ring[-1], 'dom', [(dev, (dev + 1) % 8) for dev in range(8)])  40.2 us
    ppermute x6, starting transfers between devices, passed_along(): lax.ppermute(value, axis, [(source, source + steps) for source in range(l...  32.2 us
    ppermute x6, waiting for transfers between devices, passed_along(): lax.ppermute(value, axis, [(source, source + steps) for source in range(l...  17.7 us
    dot_general x8, matrix products, barycentre_advance(): lax.dot_general(pieces[0], weights, (((1,), (1,)), ((), ())), preferred_e...  12 us
    reduce_sum x20, other arithmetic, log_advance(): jnp.sum(jnp.exp(scores - merged[:, None]), axis=1)  9.88 us
    dot_general x20, matrix products, tile_scores(): lax.dot_general(sources, target_tile, (((0,), (0,)), ((), ())), preferred...  9.87 us
  transfers between devices with their start and end apart: 13, of which 11 were waited for; matrix products, arithmetic and copies ran while one was open for 6% of the time, Pallas kernels for 0%

profile of v1, /device:TPU:5, one launch (start us, length us, event | category | flops | bytes accessed | tf_op | source)
XLA Modules:
  0.0 216.4 jit_solution(6444887649361624487)
XLA Ops:
  0.0 1.0 bitcast_convert_fusion
  1.0 1.3 collective-permute-start
  2.3 4.7 %collective-permute-done = bf16[64,512]{1,0:T(8,128)(2,1)S(1)} collective-permute-done((bf16[64,512]{1,0:T(8,128)(2,1)S(1)}, bf16[64,512]{1,0:T(8,128)(2,1)S(1)}, u32[]{:S(2)}, u32[]{:S(2)}) %collective-permute-start) | collective-permute-done | bytes 65568 | tf_op jit(solution)/shard_map/ppermute | solution.py:78
  7.0 5.8 %collective-permute-done.1 = bf16[64,512]{1,0:T(8,128)(2,1)S(1)} collective-permute-done((bf16[64,512]{1,0:T(8,128)(2,1)S(1)}, bf16[64,512]{1,0:T(8,128)(2,1)S(1)}, u32[]{:S(2)}, u32[]{:S(2)}) %collective-permute-start.1) | collective-permute-done | bytes 65568 | tf_op jit(solution)/shard_map/ppermute | solution.py:78
  12.8 5.8 %collective-permute-done.2 = bf16[64,512]{1,0:T(8,128)(2,1)S(1)} collective-permute-done((bf16[64,512]{1,0:T(8,128)(2,1)S(1)}, bf16[64,512]{1,0:T(8,128)(2,1)S(1)}, u32[]{:S(2)}, u32[]{:S(2)}) %collective-permute-start.2) | collective-permute-done | bytes 65568 | tf_op jit(solution)/shard_map/ppermute | solution.py:78
  18.6 5.8 %collective-permute-done.3 = bf16[64,512]{1,0:T(8,128)(2,1)S(1)} collective-permute-done((bf16[64,512]{1,0:T(8,128)(2,1)S(1)}, bf16[64,512]{1,0:T(8,128)(2,1)S(1)}, u32[]{:S(2)}, u32[]{:S(2)}) %collective-permute-start.3) | collective-permute-done | bytes 65568 | tf_op jit(solution)/shard_map/ppermute | solution.py:78
  24.4 5.8 %collective-permute-done.4 = bf16[64,512]{1,0:T(8,128)(2,1)S(1)} collective-permute-done((bf16[64,512]{1,0:T(8,128)(2,1)S(1)}, bf16[64,512]{1,0:T(8,128)(2,1)S(1)}, u32[]{:S(2)}, u32[]{:S(2)}) %collective-permute-start.4) | collective-permute-done | bytes 65568 | tf_op jit(solution)/shard_map/ppermute | solution.py:78
  30.2 6.5 %collective-permute-done.5 = bf16[64,512]{1,0:T(8,128)(2,1)S(1)} collective-permute-done((bf16[64,512]{1,0:T(8,128)(2,1)S(1)}, bf16[64,512]{1,0:T(8,128)(2,1)S(1)}, u32[]{:S(2)}, u32[]{:S(2)}) %collective-permute-start.5) | collective-permute-done | bytes 65568 | tf_op jit(solution)/shard_map/ppermute | solution.py:78
  36.7 5.8 %collective-permute-done.6 = bf16[64,512]{1,0:T(8,128)(2,1)S(1)} collective-permute-done((bf16[64,512]{1,0:T(8,128)(2,1)S(1)}, bf16[64,512]{1,0:T(8,128)(2,1)S(1)}, u32[]{:S(2)}, u32[]{:S(2)}) %collective-permute-start.6) | collective-permute-done | bytes 65568 | tf_op jit(solution)/shard_map/ppermute | solution.py:78
  42.6 0.9 constant_dynamic-update-slice_fusion.8
  43.6 0.8 constant_dynamic-slice_fusion.7
  44.5 10.4 %collective-permute-start.7 = (bf16[64,4096]{1,0:T(8,128)(2,1)}, bf16[64,4096]{1,0:T(8,128)(2,1)S(1)}, u32[]{:S(2)}, u32[]{:S(2)}) collective-permute-start(bf16[64,4096]{1,0:T(8,128)(2,1)} %constant_dynamic-slice_fusion.7), channel_id=1, source_target_pairs={{8,0},{16,8},{24,16},{9,1},{17,9},{25,17},{10,2},{18,10},{26,18},{... | collective-permute-start | bytes 1572872 | tf_op jit(solution)/shard_map/ppermute | solution.py:16
  54.9 1.3 collective-permute-start.8
  56.8 4.3 %while.87 = (s32[]{:T(128)}, f32[512]{0:T(512)S(1)}, f32[512]{0:T(512)S(1)}, bf16[4,64,1024]{2,1,0:T(8,128)(2,1)S(1)}, bf16[64,512]{1,0:T(8,128)(2,1)S(1)}, /*index=5*/f32[4,1024]{1,0:T(4,128)S(1)}, s32[]{:T(128)}, s32[]{:T(128)}) while((s32[]{:T(128)}, f32[512]{0:T(512)S(1)}, f32[512]{0:T(512)S(1)}, ...), condition=%wide.region_4.5_spmd.clone, body=%wide.region_1.4_spmd.clone.sunk | while | flops 70781440 | bytes 4434024 | solution.py:48
  56.8 0.5 fusion.92
  57.3 0.5 exponential_reduce_fusion.10
  57.9 0.5 fusion.92
  58.4 0.5 exponential_reduce_fusion.10
  59.5 0.5 exponential_reduce_fusion.10
  60.0 0.5 fusion.92
  60.6 0.5 exponential_reduce_fusion.10
  61.1 21.5 %all-gather = f32[8,1,512]{2,1,0:T(1,128)S(1)} all-gather(f32[1,1,512]{2,1,0:T(1,128)S(1)} %bitcast.163), channel_id=1, replica_groups=mesh['tm'=4,'dom'=8] {'dom'}, dimensions={0}, use_global_device_ids=true | all-gather | bytes 18432 | tf_op jit(solution)/shard_map/all_gather | solution.py:88
  82.6 1.3 collective-permute-start.9
  83.9 1.1 copy.11
  85.0 10.0 %collective-permute-done.9 = f32[4096]{0:T(1024)S(1)} collective-permute-done((f32[4096]{0:T(1024)S(1)}, f32[4096]{0:T(1024)S(1)}, u32[]{:S(2)}, u32[]{:S(2)}) %collective-permute-start.9) | collective-permute-done | bytes 16416 | tf_op jit(solution)/shard_map/ppermute | solution.py:16
  95.1 4.3 %while.88 = (s32[]{:T(128)}, f32[512]{0:T(512)S(1)}, f32[512]{0:T(512)S(1)}, bf16[4,64,1024]{2,1,0:T(8,128)(2,1)S(1)}, bf16[64,512]{1,0:T(8,128)(2,1)S(1)}, /*index=5*/f32[4,1024]{1,0:T(4,128)S(1)}, s32[]{:T(128)}, s32[]{:T(128)}) while((s32[]{:T(128)}, f32[512]{0:T(512)S(1)}, f32[512]{0:T(512)S(1)}, ...), condition=%wide.region_8.9_spmd.clone, body=%wide.region_5.8_spmd.clone.sunk | while | flops 70781440 | bytes 4434024 | solution.py:48
  95.1 0.5 fusion.95
  95.6 0.5 exponential_reduce_fusion.11
  96.2 0.5 fusion.95
  96.7 0.5 exponential_reduce_fusion.11
  97.8 0.5 exponential_reduce_fusion.11
  98.3 0.5 fusion.95
  98.8 0.5 exponential_reduce_fusion.11
  99.4 21.5 %all-gather.1 = f32[8,1,512]{2,1,0:T(1,128)S(1)} all-gather(f32[1,1,512]{2,1,0:T(1,128)S(1)} %bitcast.164), channel_id=1, replica_groups=mesh['tm'=4,'dom'=8] {'dom'}, dimensions={0}, use_global_device_ids=true | all-gather | bytes 18432 | tf_op jit(solution)/shard_map/all_gather | solution.py:88
  120.9 9.0 %collective-permute-start.10 = (f32[4096]{0:T(1024)S(1)}, f32[4096]{0:T(1024)S(1)}, u32[]{:S(2)}, u32[]{:S(2)}) collective-permute-start(f32[4096]{0:T(1024)S(1)} %bitcast.162), channel_id=1, source_target_pairs={{8,0},{16,8},{24,16},{9,1},{17,9},{25,17},{10,2},{18,10},{26,18},{... | collective-permute-start | bytes 49160 | tf_op jit(solution)/shard_map/ppermute | solution.py:16
  129.9 0.8 collective-permute-done.10
  130.7 4.3 %while.89 = (s32[]{:T(128)}, f32[512]{0:T(512)S(1)}, f32[512]{0:T(512)S(1)}, bf16[4,64,1024]{2,1,0:T(8,128)(2,1)S(1)}, bf16[64,512]{1,0:T(8,128)(2,1)S(1)}, /*index=5*/f32[4,1024]{1,0:T(4,128)S(1)}, s32[]{:T(128)}, s32[]{:T(128)}) while((s32[]{:T(128)}, f32[512]{0:T(512)S(1)}, f32[512]{0:T(512)S(1)}, ...), condition=%wide.region_12.13_spmd.clone, body=%wide.region_9.12_spmd.clone.sunk | while | flops 70781440 | bytes 4434024 | solution.py:48
  130.7 0.5 fusion.98
  131.2 0.5 exponential_reduce_fusion.12
  132.3 0.5 exponential_reduce_fusion.12
  133.4 0.5 exponential_reduce_fusion.12
  133.9 0.5 fusion.98
  134.5 0.5 exponential_reduce_fusion.12
  135.0 21.5 %all-gather.2 = f32[8,1,512]{2,1,0:T(1,128)S(1)} all-gather(f32[1,1,512]{2,1,0:T(1,128)S(1)} %bitcast.165), channel_id=1, replica_groups=mesh['tm'=4,'dom'=8] {'dom'}, dimensions={0}, use_global_device_ids=true | all-gather | bytes 18432 | tf_op jit(solution)/shard_map/all_gather | solution.py:88
  156.5 1.3 collective-permute-start.11
  157.9 6.4 %collective-permute-done.11 = f32[4096]{0:T(1024)S(1)} collective-permute-done((f32[4096]{0:T(1024)S(1)}, f32[4096]{0:T(1024)S(1)}, u32[]{:S(2)}, u32[]{:S(2)}) %collective-permute-start.11) | collective-permute-done | bytes 16416 | tf_op jit(solution)/shard_map/ppermute | solution.py:16
  164.3 4.3 %while.90 = (s32[]{:T(128)}, f32[512]{0:T(512)S(1)}, f32[512]{0:T(512)S(1)}, bf16[4,64,1024]{2,1,0:T(8,128)(2,1)S(1)}, bf16[64,512]{1,0:T(8,128)(2,1)S(1)}, /*index=5*/f32[4,1024]{1,0:T(4,128)S(1)}, s32[]{:T(128)}, s32[]{:T(128)}) while((s32[]{:T(128)}, f32[512]{0:T(512)S(1)}, f32[512]{0:T(512)S(1)}, ...), condition=%wide.region_16.17_spmd.clone, body=%wide.region_13.16_spmd.clone.sunk | while | flops 70781440 | bytes 4434024 | solution.py:48
  164.3 0.5 fusion.101
  168.6 21.5 %all-gather.3 = f32[8,1,512]{2,1,0:T(1,128)S(1)} all-gather(f32[1,1,512]{2,1,0:T(1,128)S(1)} %bitcast.166), channel_id=1, replica_groups=mesh['tm'=4,'dom'=8] {'dom'}, dimensions={0}, use_global_device_ids=true | all-gather | bytes 18432 | tf_op jit(solution)/shard_map/all_gather | solution.py:88
  190.1 9.0 %collective-permute-start.12 = (f32[4096]{0:T(1024)S(1)}, f32[4096]{0:T(1024)S(1)}, u32[]{:S(2)}, u32[]{:S(2)}) collective-permute-start(f32[4096]{0:T(1024)S(1)} %bitcast.159), channel_id=1, source_target_pairs={{8,0},{16,8},{24,16},{9,1},{17,9},{25,17},{10,2},{18,10},{26,18},{... | collective-permute-start | bytes 49160 | tf_op jit(solution)/shard_map/ppermute | solution.py:16
  199.1 8.7 %while.93 = (s32[]{:T(128)}, f32[64,512]{1,0:T(8,128)}, bf16[4,64,1024]{2,1,0:T(8,128)(2,1)S(1)}, bf16[64,512]{1,0:T(8,128)(2,1)S(1)}, f32[4,1024]{1,0:T(4,128)S...) while((s32[]{:T(128)}, f32[64,512]{1,0:T(8,128)}, ...), condition=%wide.region_24.25_spmd.clone, body=%wide.region_23.24_spmd.clone.sunk | while | flops 136904704 | bytes 607339 | solution.py:71
  199.2 1.5 fusion.113
  200.7 2.4 %fusion.113 = f32[64,512]{1,0:T(8,128)} fusion(bf16[64,512]{1,0:T(8,128)(2,1)S(1)} %get-tuple-element.915, f32[512]{0:T(512)S(1)} %get-tuple-element.918, f32[512]{0:T(512)S(1)} %get-tuple-element.917, f32[1024]{0:T(1024)S(1)} %bitcast.157, f32[64,512]{1,0:T(8,128)} %get-tuple-element.904, bf16[4,64,1024]{2,1,0:T(8,128)(2,1)S(1)} %get-tuple-element.914, ...), kind=kOutput, calls=%fused_computation.69.clone.1 | convolution fusion | flops 136904704 | bytes 599041 | tf_op jit(solution)/shard_map/while/body/eval_jaxpr/dot_general | solution.py:65
  203.1 2.4 %fusion.113 = f32[64,512]{1,0:T(8,128)} fusion(bf16[64,512]{1,0:T(8,128)(2,1)S(1)} %get-tuple-element.915, f32[512]{0:T(512)S(1)} %get-tuple-element.918, f32[512]{0:T(512)S(1)} %get-tuple-element.917, f32[1024]{0:T(1024)S(1)} %bitcast.157, f32[64,512]{1,0:T(8,128)} %get-tuple-element.904, bf16[4,64,1024]{2,1,0:T(8,128)(2,1)S(1)} %get-tuple-element.914, ...), kind=kOutput, calls=%fused_computation.69.clone.1 | convolution fusion | flops 136904704 | bytes 599041 | tf_op jit(solution)/shard_map/while/body/eval_jaxpr/dot_general | solution.py:65
  205.5 2.4 %fusion.113 = f32[64,512]{1,0:T(8,128)} fusion(bf16[64,512]{1,0:T(8,128)(2,1)S(1)} %get-tuple-element.915, f32[512]{0:T(512)S(1)} %get-tuple-element.918, f32[512]{0:T(512)S(1)} %get-tuple-element.917, f32[1024]{0:T(1024)S(1)} %bitcast.157, f32[64,512]{1,0:T(8,128)} %get-tuple-element.904, bf16[4,64,1024]{2,1,0:T(8,128)(2,1)S(1)} %get-tuple-element.914, ...), kind=kOutput, calls=%fused_computation.69.clone.1 | convolution fusion | flops 136904704 | bytes 599041 | tf_op jit(solution)/shard_map/while/body/eval_jaxpr/dot_general | solution.py:65
  207.9 4.3 %while.91 = (s32[]{:T(128)}, f32[512]{0:T(512)S(1)}, f32[512]{0:T(512)S(1)}, bf16[4,64,1024]{2,1,0:T(8,128)(2,1)S(1)}, bf16[64,512]{1,0:T(8,128)(2,1)S(1)}, /*index=5*/f32[4,1024]{1,0:T(4,128)S(1)}, s32[]{:T(128)}, s32[]{:T(128)}) while((s32[]{:T(128)}, f32[512]{0:T(512)S(1)}, f32[512]{0:T(512)S(1)}, ...), condition=%wide.region_20.21_spmd.clone, body=%wide.region_17.20_spmd.clone.sunk | while | flops 70781440 | bytes 4434024 | solution.py:48
  207.9 0.5 fusion.104
  211.1 0.5 fusion.104
  212.2 3.5 %while.92 = (s32[]{:T(128)}, f32[64,512]{1,0:T(8,128)S(1)}, bf16[4,64,1024]{2,1,0:T(8,128)(2,1)S(1)}, bf16[64,512]{1,0:T(8,128)(2,1)S(1)}, f32[4,1024]{1,0:T(4,1...) while((s32[]{:T(128)}, f32[64,512]{1,0:T(8,128)S(1)}, ...), condition=%wide.region_22.23_spmd.clone, body=%wide.region_21.22_spmd.clone.sunk | while | flops 136904704 | bytes 607339 | solution.py:71
  212.2 0.8 fusion.109
  213.1 0.8 fusion.109
  214.0 0.8 fusion.109
  214.8 0.8 fusion.109
  215.7 0.7 fusion.56
  (159 shorter events, 9.9 us)
Async XLA Ops:
  0.0 43.6 %copy-start = (f32[1,64,512]{2,1,0:T(8,128)S(1)}, f32[1,64,512]{2,1,0:T(8,128)}, u32[]{:S(2)}) copy-start(f32[1,64,512]{2,1,0:T(8,128)} %param.16) | copy-start | bytes 393220
  1.0 6.0 %collective-permute-start = (bf16[64,512]{1,0:T(8,128)(2,1)S(1)}, bf16[64,512]{1,0:T(8,128)(2,1)S(1)}, u32[]{:S(2)}, u32[]{:S(2)}) collective-permute-start(bf16[64,512]{1,0:T(8,128)(2,1)S(1)} %bitcast_convert_fusion), channel_id=1, source_target_pairs={{0,1},{1,2},{2,3},{3,4},{4,5},{5,6},{6,7},{7,0},{8,9},{9,10},{10,1... | collective-permute-start | bytes 196616 | tf_op jit(solution)/shard_map/ppermute | solution.py:78
  7.0 5.8 %collective-permute-start.1 = (bf16[64,512]{1,0:T(8,128)(2,1)S(1)}, bf16[64,512]{1,0:T(8,128)(2,1)S(1)}, u32[]{:S(2)}, u32[]{:S(2)}) collective-permute-start(bf16[64,512]{1,0:T(8,128)(2,1)S(1)} %collective-permute-done), channel_id=1, source_target_pairs={{0,1},{1,2},{2,3},{3,4},{4,5},{5,6},{6,7},{7,0},{8,9},{9,10},{10,1... | collective-permute-start | bytes 196616 | tf_op jit(solution)/shard_map/ppermute | solution.py:78
  12.8 5.8 %collective-permute-start.2 = (bf16[64,512]{1,0:T(8,128)(2,1)S(1)}, bf16[64,512]{1,0:T(8,128)(2,1)S(1)}, u32[]{:S(2)}, u32[]{:S(2)}) collective-permute-start(bf16[64,512]{1,0:T(8,128)(2,1)S(1)} %collective-permute-done.1), channel_id=1, source_target_pairs={{0,1},{1,2},{2,3},{3,4},{4,5},{5,6},{6,7},{7,0},{8,9},{9,10},{10,1... | collective-permute-start | bytes 196616 | tf_op jit(solution)/shard_map/ppermute | solution.py:78
  18.6 5.8 %collective-permute-start.3 = (bf16[64,512]{1,0:T(8,128)(2,1)S(1)}, bf16[64,512]{1,0:T(8,128)(2,1)S(1)}, u32[]{:S(2)}, u32[]{:S(2)}) collective-permute-start(bf16[64,512]{1,0:T(8,128)(2,1)S(1)} %collective-permute-done.2), channel_id=1, source_target_pairs={{0,1},{1,2},{2,3},{3,4},{4,5},{5,6},{6,7},{7,0},{8,9},{9,10},{10,1... | collective-permute-start | bytes 196616 | tf_op jit(solution)/shard_map/ppermute | solution.py:78
  24.4 5.8 %collective-permute-start.4 = (bf16[64,512]{1,0:T(8,128)(2,1)S(1)}, bf16[64,512]{1,0:T(8,128)(2,1)S(1)}, u32[]{:S(2)}, u32[]{:S(2)}) collective-permute-start(bf16[64,512]{1,0:T(8,128)(2,1)S(1)} %collective-permute-done.3), channel_id=1, source_target_pairs={{0,1},{1,2},{2,3},{3,4},{4,5},{5,6},{6,7},{7,0},{8,9},{9,10},{10,1... | collective-permute-start | bytes 196616 | tf_op jit(solution)/shard_map/ppermute | solution.py:78
  30.2 6.5 %collective-permute-start.5 = (bf16[64,512]{1,0:T(8,128)(2,1)S(1)}, bf16[64,512]{1,0:T(8,128)(2,1)S(1)}, u32[]{:S(2)}, u32[]{:S(2)}) collective-permute-start(bf16[64,512]{1,0:T(8,128)(2,1)S(1)} %collective-permute-done.4), channel_id=1, source_target_pairs={{0,1},{1,2},{2,3},{3,4},{4,5},{5,6},{6,7},{7,0},{8,9},{9,10},{10,1... | collective-permute-start | bytes 196616 | tf_op jit(solution)/shard_map/ppermute | solution.py:78
  36.7 5.8 %collective-permute-start.6 = (bf16[64,512]{1,0:T(8,128)(2,1)S(1)}, bf16[64,512]{1,0:T(8,128)(2,1)S(1)}, u32[]{:S(2)}, u32[]{:S(2)}) collective-permute-start(bf16[64,512]{1,0:T(8,128)(2,1)S(1)} %collective-permute-done.5), channel_id=1, source_target_pairs={{0,1},{1,2},{2,3},{3,4},{4,5},{5,6},{6,7},{7,0},{8,9},{9,10},{10,1... | collective-permute-start | bytes 196616 | tf_op jit(solution)/shard_map/ppermute | solution.py:78
  44.5 12.1 %collective-permute-start.7 = (bf16[64,4096]{1,0:T(8,128)(2,1)}, bf16[64,4096]{1,0:T(8,128)(2,1)S(1)}, u32[]{:S(2)}, u32[]{:S(2)}) collective-permute-start(bf16[64,4096]{1,0:T(8,128)(2,1)} %constant_dynamic-slice_fusion.7), channel_id=1, source_target_pairs={{8,0},{16,8},{24,16},{9,1},{17,9},{25,17},{10,2},{18,10},{26,18},{... | collective-permute-start | bytes 1572872 | tf_op jit(solution)/shard_map/ppermute | solution.py:16
  54.9 29.0 %collective-permute-start.8 = (bf16[64,4096]{1,0:T(8,128)(2,1)}, bf16[64,4096]{1,0:T(8,128)(2,1)}, u32[]{:S(2)}, u32[]{:S(2)}) collective-permute-start(bf16[64,4096]{1,0:T(8,128)(2,1)} %constant_dynamic-slice_fusion.7), channel_id=1, source_target_pairs={{0,8},{8,16},{16,24},{1,9},{9,17},{17,25},{2,10},{10,18},{18,26},{... | collective-permute-start | bytes 1572872 | tf_op jit(solution)/shard_map/ppermute | solution.py:16
  82.6 12.4 %collective-permute-start.9 = (f32[4096]{0:T(1024)S(1)}, f32[4096]{0:T(1024)S(1)}, u32[]{:S(2)}, u32[]{:S(2)}) collective-permute-start(f32[4096]{0:T(1024)S(1)} %bitcast.161), channel_id=1, source_target_pairs={{0,8},{8,16},{16,24},{1,9},{9,17},{17,25},{2,10},{10,18},{18,26},{... | collective-permute-start | bytes 49160 | tf_op jit(solution)/shard_map/ppermute | solution.py:16
  120.9 9.8 %collective-permute-start.10 = (f32[4096]{0:T(1024)S(1)}, f32[4096]{0:T(1024)S(1)}, u32[]{:S(2)}, u32[]{:S(2)}) collective-permute-start(f32[4096]{0:T(1024)S(1)} %bitcast.162), channel_id=1, source_target_pairs={{8,0},{16,8},{24,16},{9,1},{17,9},{25,17},{10,2},{18,10},{26,18},{... | collective-permute-start | bytes 49160 | tf_op jit(solution)/shard_map/ppermute | solution.py:16
  156.5 7.8 %collective-permute-start.11 = (f32[4096]{0:T(1024)S(1)}, f32[4096]{0:T(1024)S(1)}, u32[]{:S(2)}, u32[]{:S(2)}) collective-permute-start(f32[4096]{0:T(1024)S(1)} %bitcast.160), channel_id=1, source_target_pairs={{0,8},{8,16},{16,24},{1,9},{9,17},{17,25},{2,10},{10,18},{18,26},{... | collective-permute-start | bytes 49160 | tf_op jit(solution)/shard_map/ppermute | solution.py:16
  190.1 17.7 %collective-permute-start.12 = (f32[4096]{0:T(1024)S(1)}, f32[4096]{0:T(1024)S(1)}, u32[]{:S(2)}, u32[]{:S(2)}) collective-permute-start(f32[4096]{0:T(1024)S(1)} %bitcast.159), channel_id=1, source_target_pairs={{8,0},{16,8},{24,16},{9,1},{17,9},{25,17},{10,2},{18,10},{26,18},{... | collective-permute-start | bytes 49160 | tf_op jit(solution)/shard_map/ppermute | solution.py:16
  212.2 3.5 %copy-start.1 = (f32[1,64,512]{2,1,0:T(8,128)S(1)}, f32[1,64,512]{2,1,0:T(8,128)}, u32[]{:S(2)}) copy-start(f32[1,64,512]{2,1,0:T(8,128)} %param.17) | copy-start | bytes 393220
  212.2 3.5 %copy-start.2 = (f32[64,512]{1,0:T(8,128)S(1)}, f32[64,512]{1,0:T(8,128)}, u32[]{:S(2)}) copy-start(f32[64,512]{1,0:T(8,128)} %get-tuple-element.255) | copy-start | bytes 393220
